TPU v7x, 256 devices: a whole 4x4x8 slice. The times are simulated.
256 devices in a mesh: seq: 128 (over x_lo, z, y, core), tp: 2 (over x_hi).
Axes of the slice: x: 4 (x_hi: 2, x_lo: 2; x = x_hi * 2 + x_lo), y: 4, z: 8, core: 2. Of those that a mesh axis runs over, the one named last changes fastest.
Arguments:
- tokens: bfloat16 [32768, 1024], P('seq', 'tp')
- w_query: bfloat16 [1024, 1024], P(None, 'tp'), may hold values from -0.1875 to 0.1875
- w_key: bfloat16 [1024, 1024], P(None, 'tp'), may hold values from -0.1875 to 0.1875
- w_value: bfloat16 [1024, 1024], P(None, 'tp'), may hold values from -0.1875 to 0.1875
- w_out: bfloat16 [1024, 1024], P('tp'), may hold values from -0.1875 to 0.1875
- grad_out: bfloat16 [32768, 1024], P('seq', 'tp'), may hold values from -6 to 6
- block_sky: int32 [128], replicated, may hold values from 0 to 127, as said below
- neighbours: int32 [128, 3], replicated, may hold values from 0 to 127, as said below
- valid_count: int32 [128], replicated, may hold values from 32 to 256
Outputs:
- outputs: bfloat16 [32768, 1024], P('seq', 'tp')
- input_grads: bfloat16 [32768, 1024], P('seq', 'tp')
Inputs may be any that keep to these rules, and one draw needn't show every extreme that they name: `block_sky`: a permutation; slot s lies on the seq index s. Three different sky blocks other than the block itself; for the block in slot s the slots of its neighbours lie on three different seq indices at distance 1 or 2 from that of slot s, counted modulo the size of seq.
All inputs are finite; a program needn't handle non-finite values.
Results may differ from a plain program's by a relative error of at most 0.018.
The roundings to bfloat16 on the way count: a program that leaves them out, or rounds other values in their place, can miss the bound.
Values may be sent and summed in bfloat16 or wider, within the bound.
A program may use at most 128 MiB of HBM per device.

v0:
```python
import jax
import jax.numpy as jnp
from jax import lax
from jax.sharding import PartitionSpec as P

HD = 64
BLK = 256


def from_behind(value, axis, steps):
    count = lax.axis_size(axis)
    pairs = [(source, (source + steps) % count) for source in range(count)]
    return lax.ppermute(value, axis, pairs)


def invert(block_sky):
    numbers = jnp.arange(block_sky.shape[0], dtype=jnp.int32)
    return jnp.sum(jnp.where(block_sky[:, None] == numbers[None, :], numbers[:, None], 0), axis=0)


def lookup(table, index):
    numbers = jnp.arange(table.shape[0], dtype=jnp.int32)
    return jnp.sum(jnp.where(index[..., None] == numbers, table, 0), axis=-1)


def layout(slot_ids, block_sky, neighbours, slot_of):
    sky_ids = lookup(block_sky, slot_ids)
    numbers = jnp.arange(block_sky.shape[0], dtype=jnp.int32)
    matches = sky_ids[:, None] == numbers[None, :]
    near_sky = jnp.sum(jnp.where(matches[:, :, None], neighbours[None, :, :], 0), axis=1)
    near_slots = lookup(slot_of, near_sky)
    key_sky = jnp.concatenate([sky_ids[:, None], near_sky], axis=1)
    return (near_slots, key_sky)


def signed(distance, device_count):
    wrapped = distance % device_count
    return jnp.where(wrapped > device_count // 2, wrapped - device_count, wrapped)


def spread(block):
    head_count = block.shape[1] // HD
    return block.reshape(block.shape[0], head_count, HD)


def score_heads(block_rows, block_keys, block_mask):
    scores = jnp.einsum(
        "qhd,khd->hqk", spread(block_rows), spread(block_keys), preferred_element_type=jnp.float32
    )
    scores = scores * HD ** (-0.5)
    return jnp.where(block_mask[None, None, :], scores, -jnp.inf)


def forward_block(operands):
    block_rows, block_keys, block_values, block_mask = operands
    scores = score_heads(block_rows, block_keys, block_mask)
    row_max = jnp.max(scores, axis=-1, keepdims=True)
    log_total = row_max + jnp.log(jnp.sum(jnp.exp(scores - row_max), axis=-1, keepdims=True))
    weights = jnp.exp(scores - log_total).astype(jnp.bfloat16)
    attended = jnp.einsum(
        "hqk,khd->qhd", weights, spread(block_values), preferred_element_type=jnp.float32
    )
    return (attended.reshape(block_rows.shape[0], -1).astype(jnp.bfloat16), log_total[:, :, 0])


def gradient_terms(block_rows, block_keys, block_values, block_grads, block_total, block_mask):
    scores = score_heads(block_rows, block_keys, block_mask)
    probabilities = jnp.exp(scores - block_total[:, :, None])
    weights = probabilities.astype(jnp.bfloat16)
    prob_grads = jnp.einsum(
        "qhd,khd->hqk",
        spread(block_grads),
        spread(block_values),
        preferred_element_type=jnp.float32,
    )
    row_delta = jnp.sum(probabilities * prob_grads, axis=-1)
    score_grads = (probabilities * (prob_grads - row_delta[:, :, None]) * HD ** (-0.5)).astype(
        jnp.bfloat16
    )
    return (weights, score_grads, row_delta)


def key_terms(weights, score_grads, block_rows, block_grads):
    key_part = jnp.einsum(
        "hqk,qhd->khd", score_grads, spread(block_rows), preferred_element_type=jnp.float32
    )
    value_part = jnp.einsum(
        "hqk,qhd->khd", weights, spread(block_grads), preferred_element_type=jnp.float32
    )
    return (key_part.reshape(key_part.shape[0], -1), value_part.reshape(value_part.shape[0], -1))


def backward_block(operands):
    block_rows, block_keys, block_values, block_grads, block_total, block_mask = operands
    weights, score_grads, row_delta = gradient_terms(
        block_rows, block_keys, block_values, block_grads, block_total, block_mask
    )
    row_grads = jnp.einsum(
        "hqk,khd->qhd", score_grads, spread(block_keys), preferred_element_type=jnp.float32
    )
    row_grads = row_grads.reshape(block_rows.shape[0], -1).astype(jnp.bfloat16)
    key_part, value_part = key_terms(weights, score_grads, block_rows, block_grads)
    return (row_grads, key_part, value_part, row_delta)


def body(tokens, w_query, w_key, w_value, w_out, grad_out, block_sky, neighbours, valid_count):
    whole = lax.all_gather(tokens, "tp", axis=1, tiled=True)
    queries = jnp.dot(whole, w_query, preferred_element_type=jnp.float32).astype(jnp.bfloat16)
    key_rows = jnp.dot(whole, w_key, preferred_element_type=jnp.float32).astype(jnp.bfloat16)
    value_rows = jnp.dot(whole, w_value, preferred_element_type=jnp.float32).astype(jnp.bfloat16)
    width = queries.shape[1]
    group_width = width // 2
    group_heads = group_width // HD
    local_blocks = queries.shape[0] // BLK
    device = lax.axis_index("seq")
    device_count = lax.axis_size("seq")
    local_numbers = jnp.arange(local_blocks, dtype=jnp.int32)
    key_value = jnp.concatenate([key_rows, value_rows], axis=1)
    received = {}
    for offset in (-2, -1, 1, 2):
        received[offset] = from_behind(key_value, "seq", -offset)
    window = jnp.stack([received[-2], received[-1], key_value, received[1], received[2]])
    slot_of = invert(block_sky)
    own_slots = device * local_blocks + local_numbers
    near_slots, key_sky = layout(own_slots, block_sky, neighbours, slot_of)
    distance = signed(near_slots // local_blocks - device, device_count)
    near_index = (distance + 2) * local_blocks + near_slots % local_blocks
    window_index = jnp.concatenate(
        [(2 * local_blocks + local_numbers)[:, None], near_index], axis=1
    )
    positions = jnp.arange(BLK, dtype=jnp.int32)
    key_counts = lookup(valid_count, key_sky)
    key_mask = (positions[None, None, :] < key_counts[:, :, None]).reshape(local_blocks, 4 * BLK)
    gathered = window[window_index].reshape(local_blocks, 4 * BLK, 2 * width)
    q_blocks = queries.reshape(local_blocks, BLK, width)
    attended_parts = []
    total_parts = []
    for group in range(2):
        lower = group * group_width
        upper = lower + group_width
        attended_group, total_group = lax.map(
            forward_block,
            (
                q_blocks[:, :, lower:upper],
                gathered[:, :, lower:upper],
                gathered[:, :, width + lower : width + upper],
                key_mask,
            ),
        )
        attended_parts.append(attended_group)
        total_parts.append(total_group)
    attended = jnp.concatenate(attended_parts, axis=2).reshape(-1, width)
    log_total = jnp.concatenate(total_parts, axis=1)
    partial_out = jnp.dot(attended, w_out, preferred_element_type=jnp.float32)
    outputs = lax.psum_scatter(
        partial_out.astype(jnp.bfloat16), "tp", scatter_dimension=1, tiled=True
    )
    grad_whole = lax.all_gather(grad_out, "tp", axis=1, tiled=True)
    grad_rows = jnp.dot(grad_whole, w_out.T, preferred_element_type=jnp.float32).astype(
        jnp.bfloat16
    )
    g_blocks = grad_rows.reshape(local_blocks, BLK, width)
    row_parts, key_parts, value_parts = ([], [], [])
    for group in range(2):
        lower = group * group_width
        upper = lower + group_width
        head_lower = group * group_heads
        row_group, key_group, value_group, delta_group = lax.map(
            backward_block,
            (
                q_blocks[:, :, lower:upper],
                gathered[:, :, lower:upper],
                gathered[:, :, width + lower : width + upper],
                g_blocks[:, :, lower:upper],
                log_total[:, head_lower : head_lower + group_heads],
                key_mask,
            ),
        )
        row_parts.append(row_group)
        key_parts.append(key_group)
        value_parts.append(value_group)
    query_grads = jnp.concatenate(row_parts, axis=2).reshape(-1, width)
    combined = jnp.concatenate(key_parts + value_parts, axis=2).reshape(
        local_blocks, 4, BLK, 2 * width
    )
    placing = (
        window_index[:, :, None] == jnp.arange(5 * local_blocks, dtype=jnp.int32)[None, None, :]
    ).astype(jnp.float32)
    window_grads = jnp.einsum("bjw,bjtc->wtc", placing, combined, precision=lax.Precision.HIGHEST)
    summed = window_grads[2 * local_blocks : 3 * local_blocks].reshape(-1, 2 * width)
    for offset in (-2, -1, 1, 2):
        start = (offset + 2) * local_blocks
        returned = window_grads[start : start + local_blocks].reshape(-1, 2 * width)
        summed = summed + from_behind(returned.astype(jnp.bfloat16), "seq", offset).astype(
            returned.dtype
        )
    key_grads = summed[:, :width].astype(jnp.bfloat16)
    value_grads = summed[:, width:].astype(jnp.bfloat16)
    partial_in = jnp.dot(query_grads, w_query.T, preferred_element_type=jnp.float32)
    partial_in = partial_in + jnp.dot(key_grads, w_key.T, preferred_element_type=jnp.float32)
    partial_in = partial_in + jnp.dot(value_grads, w_value.T, preferred_element_type=jnp.float32)
    input_grads = lax.psum_scatter(
        partial_in.astype(jnp.bfloat16), "tp", scatter_dimension=1, tiled=True
    )
    return (outputs, input_grads)


def solution(mesh):
    placed = (
        P("seq", "tp"),
        P(None, "tp"),
        P(None, "tp"),
        P(None, "tp"),
        P("tp", None),
        P("seq", "tp"),
        P(),
        P(),
        P(),
    )
    return jax.shard_map(
        body,
        mesh=mesh,
        in_specs=placed,
        out_specs=(P("seq", "tp"), P("seq", "tp")),
        check_vma=False,
    )
```

profile of v0, /device:TPU:1, one launch (start us, length us, event | category | flops | bytes accessed | tf_op | source)
XLA Modules:
  0.0 226.5 jit_solution(4011747869392042063)
XLA Ops:
  7.3 9.7 %all_gather.6 = bf16[256,1024]{1,0:T(8,128)(2,1)S(1)} all-gather(bf16[256,512]{1,0:T(8,128)(2,1)} %param.9), channel_id=1, replica_groups=mesh['seq'=128,'tp'=2] {'tp'}, dimensions={1}, use_global_device_ids=true | all-gather | bytes 786432 | tf_op jit(solution)/shard_map/all_gather | solution.py:107
  21.2 2.5 %collective-permute-start.2 = (bf16[256,1024]{1,0:T(8,128)(2,1)}, bf16[256,1024]{1,0:T(8,128)(2,1)}, u32[]{:S(2)}, u32[]{:S(2)}) collective-permute-start(bf16[256,1024]{1,0:T(8,128)(2,1)} %pad_maximum_fusion), channel_id=1, source_target_pairs={{0,254},{2,0},{4,2},{6,4},{8,6},{10,8},{12,10},{14,12},{16,14},{18... | collective-permute-start | bytes 1572872 | tf_op jit(solution)/shard_map/ppermute | solution.py:13
  23.6 8.9 %collective-permute-start.3 = (bf16[256,1024]{1,0:T(8,128)(2,1)}, bf16[256,1024]{1,0:T(8,128)(2,1)}, u32[]{:S(2)}, u32[]{:S(2)}) collective-permute-start(bf16[256,1024]{1,0:T(8,128)(2,1)} %pad_maximum_fusion), channel_id=1, source_target_pairs={{0,252},{2,254},{4,0},{6,2},{8,4},{10,6},{12,8},{14,10},{16,12},{1... | collective-permute-start | bytes 1572872 | tf_op jit(solution)/shard_map/ppermute | solution.py:13
  35.3 10.1 %all_gather.7 = bf16[256,1024]{1,0:T(8,128)(2,1)S(1)} all-gather(bf16[256,512]{1,0:T(8,128)(2,1)S(1)} %copy-done.12), channel_id=1, replica_groups=mesh['seq'=128,'tp'=2] {'tp'}, dimensions={1}, use_global_device_ids=true | all-gather | bytes 786432 | tf_op jit(solution)/shard_map/all_gather | solution.py:158
  48.1 8.5 %collective-permute-done = bf16[256,1024]{1,0:T(8,128)(2,1)} collective-permute-done((bf16[256,1024]{1,0:T(8,128)(2,1)}, bf16[256,1024]{1,0:T(8,128)(2,1)}, u32[]{:S(2)}, u32[]{:S(2)}) %collective-permute-start) | collective-permute-done | bytes 524320 | tf_op jit(solution)/shard_map/ppermute | solution.py:13
  65.0 2.4 %gather_fusion = bf16[4,256,1024]{2,1,0:T(8,128)(2,1)S(1)} fusion(bf16[5,256,1024]{2,1,0:T(8,128)(2,1)} %bitcast_dynamic-update-slice_fusion, s32[1024]{0:T(1024)S(1)} %pad_clamp_fusion), kind=kCustom, calls=%fused_computation | custom fusion | bytes 4194320 | tf_op jit(solution)/shard_map/gather | solution.py:134
  72.8 2.7 %fusion.113 = f32[4,256,1024]{2,1,0:T(8,128)} fusion(bf16[256,4,64]{0,2,1:T(8,128)(2,1)S(1)} %bitcast.141, bf16[1024,4,64]{0,2,1:T(8,128)(2,1)S(1)} %bitcast.131), kind=kOutput, calls=%fused_computation.139 | convolution fusion | flops 134217728 | bytes 4849664 | tf_op jit(solution)/shard_map/while/body/eval_jaxpr/qhd,khd->hqk/dot_general | solution.py:70
  80.9 2.0 convolution_bitcast_fusion.1
  83.1 2.7 %fusion.114 = f32[4,256,1024]{2,1,0:T(8,128)} fusion(bf16[256,4,64]{0,2,1:T(8,128)(2,1)S(1)} %bitcast.139, bf16[1024,4,64]{0,2,1:T(8,128)(2,1)S(1)} %bitcast.133), kind=kOutput, calls=%fused_computation.140 | convolution fusion | flops 134217728 | bytes 4849664 | tf_op jit(solution)/shard_map/while/body/eval_jaxpr/qhd,khd->hqk/dot_general | solution.py:70
  88.6 24.1 %fusion.37 = f32[1024,4,64]{0,2,1:T(8,128)} fusion(bf16[256,4,64]{0,2,1:T(8,128)(2,1)S(1)} %bitcast.138, f32[4,256,1024]{2,1,0:T(8,128)} %fusion.113, f32[4,256,1024]{2,1,0:T(8,128)} %copy-done.6, f32[4,256]{1,0:T(4,128)S(1)} %get-tuple-element.104, pred[1024]{0:T(1024)(128)(4,1)S(1)} %lt.55), kind=kOutput, calls=%fused_computation.34 | convolution fusion | flops 145754112 | bytes 9573376 | tf_op jit(solution)/shard_map/while/body/eval_jaxpr/hqk,qhd->khd/dot_general | solution.py:84
  112.7 12.7 %fusion.34 = f32[1024,4,64]{0,2,1:T(8,128)} fusion(bf16[256,4,64]{0,2,1:T(8,128)(2,1)S(1)} %bitcast.148, f32[4,256,1024]{2,1,0:T(8,128)} %fusion.114, f32[4,256,1024]{2,1,0:T(8,128)} %copy-done.1, f32[4,256]{1,0:T(4,128)S(1)} %get-tuple-element.103, pred[1024]{0:T(1024)(128)(4,1)S(1)} %lt.55), kind=kOutput, calls=%fused_computation.33 | convolution fusion | flops 145754112 | bytes 9573376 | tf_op jit(solution)/shard_map/while/body/eval_jaxpr/hqk,qhd->khd/dot_general | solution.py:84
  126.6 2.7 %concatenate.69 = f32[4,256,256]{1,0,2:T(4,128)} reshape(f32[1024,4,64]{0,2,1:T(8,128)} %fusion.34) | data formatting | bytes 2097152 | tf_op jit(solution)/shard_map/concatenate | solution.py:183
  130.9 2.7 %concatenate.70 = f32[4,256,256]{1,0,2:T(4,128)} reshape(f32[1024,4,64]{0,2,1:T(8,128)} %convolution_bitcast_fusion.1) | data formatting | bytes 2097152 | tf_op jit(solution)/shard_map/concatenate | solution.py:183
  133.5 2.3 %copy.95 = f32[4,256,256]{2,0,1:T(4,128)} copy(f32[4,256,256]{1,0,2:T(4,128)} %concatenate.70) | data formatting | bytes 2097152 | tf_op jit(solution)/shard_map/concatenate | solution.py:183
  135.9 2.7 %concatenate.68 = f32[4,256,256]{1,0,2:T(4,128)} reshape(f32[1024,4,64]{0,2,1:T(8,128)} %fusion.37) | data formatting | bytes 2097152 | tf_op jit(solution)/shard_map/concatenate | solution.py:183
  138.6 2.2 copy.93
  140.8 10.9 %fusion.112 = (bf16[5,256,1024]{2,0,1:T(8,128)(2,1)S(1)}, f32[5,256,1024]{2,0,1:T(8,128)}) fusion(f32[4,256,256]{2,0,1:T(4,128)S(1)} %copy.96, f32[4,256,256]{2,0,1:T(4,128)} %copy.95, f32[4,256,256]{2,0,1:T(4,128)S(1)} %copy.94, f32[4,256,256]{2,0,1:T(4,128)} %copy.93, s32[4]{0:T(128)S(1)} %add_bitcast_fusion.1), kind=kOutput, calls=%fused_computation.138 | convolution fusion | flops 67371024 | bytes 12058640 | tf_op jit(solution)/shard_map/bjw,bjtc->wtc/dot_general | solution.py:189
  151.7 3.0 %fusion.108 = (bf16[1,256,1024]{2,0,1:T(2,128)(2,1)S(1)}, bf16[1,256,1024]{2,0,1:T(2,128)(2,1)S(1)}, bf16[1,256,1024]{2,0,1:T(2,128)(2,1)S(1)}, bf16[1,256,1024]{2,0,1:T(2,128)(2,1)S(1)}) fusion(bf16[5,256,1024]{2,0,1:T(8,128)(2,1)S(1)} %get-tuple-element.101), kind=kLoop, calls=%fused_computation.134 | loop fusion | bytes 4194304 | tf_op jit(solution)/shard_map/slice | solution.py:193
  158.9 5.7 %collective-permute-start.4 = (bf16[256,1024]{1,0:T(8,128)(2,1)S(1)}, bf16[256,1024]{1,0:T(8,128)(2,1)}, u32[]{:S(2)}, u32[]{:S(2)}) collective-permute-start(bf16[256,1024]{1,0:T(8,128)(2,1)S(1)} %bitcast.135), channel_id=1, source_target_pairs={{0,252},{2,254},{4,0},{6,2},{8,4},{10,6},{12,8},{14,10},{16,12},{1... | collective-permute-start | bytes 1572872 | tf_op jit(solution)/shard_map/ppermute | solution.py:13
  165.9 11.4 %fusion.48 = bf16[4,64,256]{2,1,0:T(8,128)(2,1)S(1)} fusion(bf16[1024,4,64]{0,2,1:T(8,128)(2,1)S(1)} %bitcast.130, f32[4,256,1024]{2,1,0:T(8,128)} %fusion.113, f32[4,256]{1,0:T(4,128)S(1)} %get-tuple-element.104, f32[4,256,1024]{2,1,0:T(8,128)} %copy-done.6, pred[1024]{0:T(1024)(128)(4,1)S(1)} %lt.55), kind=kOutput, calls=%fused_computation.50 | convolution fusion | flops 145819648 | bytes 9049088 | tf_op jit(solution)/shard_map/while/body/eval_jaxpr/hqk,khd->qhd/dot_general | solution.py:98
  177.4 11.6 %fusion.45 = bf16[4,64,256]{2,1,0:T(8,128)(2,1)S(1)} fusion(bf16[1024,4,64]{0,2,1:T(8,128)(2,1)} %bitcast.144, f32[4,256,1024]{2,1,0:T(8,128)} %fusion.114, f32[4,256]{1,0:T(4,128)S(1)} %get-tuple-element.103, f32[4,256,1024]{2,1,0:T(8,128)} %copy-done.1, pred[1024]{0:T(1024)(128)(4,1)S(1)} %lt.55), kind=kOutput, calls=%fused_computation.49 | convolution fusion | flops 145819648 | bytes 9049088 | tf_op jit(solution)/shard_map/while/body/eval_jaxpr/hqk,khd->qhd/dot_general | solution.py:98
  189.6 4.7 %slice.82 = f32[1,256,1024]{2,0,1:T(1,128)S(1)} slice(f32[5,256,1024]{2,0,1:T(8,128)} %get-tuple-element.102), slice={[2:3], [0:256], [0:1024]} | slice | bytes 2097152 | tf_op jit(solution)/shard_map/slice | solution.py:190
  194.3 2.1 fusion.54
  198.2 21.2 %reduce-scatter.5.cloned.1.call-done = bf16[256,512]{1,0:T(8,128)(2,1)} async-done(((bf16[256,1024]{1,0:T(8,128)(2,1)}), bf16[256,512]{1,0:T(8,128)(2,1)}) %reduce-scatter.5.cloned.1.call-update) | async-done | bytes 262160 | tf_op jit(solution)/shard_map/reduce_scatter | solution.py:202
  (108 shorter events, 42.1 us)
Async XLA Ops:
  7.2 38.2 %copy-start = (bf16[512,1024]{1,0:T(8,128)(2,1)S(1)}, bf16[512,1024]{1,0:T(8,128)(2,1)}, u32[]{:S(2)}) copy-start(bf16[512,1024]{1,0:T(8,128)(2,1)} %param.13) | copy-start | bytes 3145732
  7.2 25.8 %copy-start.15 = (s32[128]{0:T(128)S(1)}, s32[128]{0:T(128)}, u32[]{:S(2)}) copy-start(s32[128]{0:T(128)} %param.15) | copy-start | bytes 1540
  7.2 27.2 %copy-start.14 = (s32[128,3]{0,1:T(4,128)S(1)}, s32[128,3]{0,1:T(4,128)}, u32[]{:S(2)}) copy-start(s32[128,3]{0,1:T(4,128)} %param.16) | copy-start | bytes 4612
  7.2 27.6 %copy-start.3 = (bf16[1024,512]{1,0:T(8,128)(2,1)S(1)}, bf16[1024,512]{1,0:T(8,128)(2,1)}, u32[]{:S(2)}) copy-start(bf16[1024,512]{1,0:T(8,128)(2,1)} %param.10) | copy-start | bytes 3145732
  7.2 28.0 %copy-start.12 = (bf16[256,512]{1,0:T(8,128)(2,1)S(1)}, bf16[256,512]{1,0:T(8,128)(2,1)}, u32[]{:S(2)}) copy-start(bf16[256,512]{1,0:T(8,128)(2,1)} %param.14) | copy-start | bytes 786436
  7.2 191.0 %reduce-scatter.3.cloned.1.call-start = ((), (), s32[]{:S(2)}) async-start(), calls=%async_computation.2 | async-start | bytes 786432 | tf_op jit(solution)/shard_map/reduce_scatter | solution.py:155
  18.6 28.0 %copy-start.16 = (s32[128]{0:T(128)S(1)}, s32[128]{0:T(128)}, u32[]{:S(2)}) copy-start(s32[128]{0:T(128)} %param.17) | copy-start | bytes 1540
  21.2 40.1 %collective-permute-start.2 = (bf16[256,1024]{1,0:T(8,128)(2,1)}, bf16[256,1024]{1,0:T(8,128)(2,1)}, u32[]{:S(2)}, u32[]{:S(2)}) collective-permute-start(bf16[256,1024]{1,0:T(8,128)(2,1)} %pad_maximum_fusion), channel_id=1, source_target_pairs={{0,254},{2,0},{4,2},{6,4},{8,6},{10,8},{12,10},{14,12},{16,14},{18... | collective-permute-start | bytes 1572872 | tf_op jit(solution)/shard_map/ppermute | solution.py:13
  23.6 39.5 %collective-permute-start.3 = (bf16[256,1024]{1,0:T(8,128)(2,1)}, bf16[256,1024]{1,0:T(8,128)(2,1)}, u32[]{:S(2)}, u32[]{:S(2)}) collective-permute-start(bf16[256,1024]{1,0:T(8,128)(2,1)} %pad_maximum_fusion), channel_id=1, source_target_pairs={{0,252},{2,254},{4,0},{6,2},{8,4},{10,6},{12,8},{14,10},{16,12},{1... | collective-permute-start | bytes 1572872 | tf_op jit(solution)/shard_map/ppermute | solution.py:13
  32.5 25.9 %collective-permute-start.1 = (bf16[256,1024]{1,0:T(8,128)(2,1)}, bf16[256,1024]{1,0:T(8,128)(2,1)}, u32[]{:S(2)}, u32[]{:S(2)}) collective-permute-start(bf16[256,1024]{1,0:T(8,128)(2,1)} %pad_maximum_fusion), channel_id=1, source_target_pairs={{0,2},{2,4},{4,6},{6,8},{8,10},{10,12},{12,14},{14,16},{16,18},{18... | collective-permute-start | bytes 1572872 | tf_op jit(solution)/shard_map/ppermute | solution.py:13
  33.0 23.6 %collective-permute-start = (bf16[256,1024]{1,0:T(8,128)(2,1)}, bf16[256,1024]{1,0:T(8,128)(2,1)}, u32[]{:S(2)}, u32[]{:S(2)}) collective-permute-start(bf16[256,1024]{1,0:T(8,128)(2,1)} %pad_maximum_fusion), channel_id=1, source_target_pairs={{0,4},{2,6},{4,8},{6,10},{8,12},{10,14},{12,16},{14,18},{16,20},{1... | collective-permute-start | bytes 1572872 | tf_op jit(solution)/shard_map/ppermute | solution.py:13
  71.4 5.0 %copy-start.11 = (bf16[1,1024,256]{1,2,0:T(8,128)(2,1)}, bf16[1,1024,256]{1,2,0:T(8,128)(2,1)S(1)}, u32[]{:S(2)}) copy-start(bf16[1,1024,256]{1,2,0:T(8,128)(2,1)S(1)} %copy.90) | copy-start | bytes 1572868
  72.8 3.6 %copy-start.13 = (bf16[1,256,256]{1,2,0:T(8,128)(2,1)S(1)}, bf16[1,256,256]{1,2,0:T(8,128)(2,1)}, u32[]{:S(2)}) copy-start(bf16[1,256,256]{1,2,0:T(8,128)(2,1)} %copy.89) | copy-start | bytes 393220
  76.4 4.5 %copy-start.6 = (f32[4,256,1024]{2,1,0:T(8,128)}, f32[4,256,1024]{2,1,0:T(8,128)S(1)}, u32[]{:S(2)}) copy-start(f32[4,256,1024]{2,1,0:T(8,128)S(1)} %get-tuple-element.99) | copy-start | bytes 12582916
  154.8 9.8 %copy-start.17 = (bf16[4,64,256]{2,1,0:T(8,128)(2,1)S(1)}, bf16[4,64,256]{2,1,0:T(8,128)(2,1)}, u32[]{:S(2)}) copy-start(bf16[4,64,256]{2,1,0:T(8,128)(2,1)} %convolution_convert_fusion.6) | copy-start | bytes 393220
  154.8 11.1 %copy-start.9 = (bf16[1,1024,256]{1,2,0:T(8,128)(2,1)S(1)}, bf16[1,1024,256]{1,2,0:T(8,128)(2,1)}, u32[]{:S(2)}) copy-start(bf16[1,1024,256]{1,2,0:T(8,128)(2,1)} %copy-done.8) | copy-start | bytes 1572868
  157.2 37.1 %collective-permute-start.5 = (bf16[256,1024]{1,0:T(8,128)(2,1)}, bf16[256,1024]{1,0:T(8,128)(2,1)}, u32[]{:S(2)}, u32[]{:S(2)}) collective-permute-start(bf16[256,1024]{1,0:T(8,128)(2,1)} %bitcast.126), channel_id=1, source_target_pairs={{0,254},{2,0},{4,2},{6,4},{8,6},{10,8},{12,10},{14,12},{16,14},{18... | collective-permute-start | bytes 1572872 | tf_op jit(solution)/shard_map/ppermute | solution.py:13
  157.2 37.1 %collective-permute-start.6 = (bf16[256,1024]{1,0:T(8,128)(2,1)}, bf16[256,1024]{1,0:T(8,128)(2,1)}, u32[]{:S(2)}, u32[]{:S(2)}) collective-permute-start(bf16[256,1024]{1,0:T(8,128)(2,1)} %bitcast.125), channel_id=1, source_target_pairs={{0,2},{2,4},{4,6},{6,8},{8,10},{10,12},{12,14},{14,16},{16,18},{18... | collective-permute-start | bytes 1572872 | tf_op jit(solution)/shard_map/ppermute | solution.py:13
  158.9 35.3 %collective-permute-start.7 = (bf16[256,1024]{1,0:T(8,128)(2,1)S(1)}, bf16[256,1024]{1,0:T(8,128)(2,1)}, u32[]{:S(2)}, u32[]{:S(2)}) collective-permute-start(bf16[256,1024]{1,0:T(8,128)(2,1)S(1)} %bitcast.136), channel_id=1, source_target_pairs={{0,4},{2,6},{4,8},{6,10},{8,12},{10,14},{12,16},{14,18},{16,20},{1... | collective-permute-start | bytes 1572872 | tf_op jit(solution)/shard_map/ppermute | solution.py:13
  158.9 35.3 %collective-permute-start.4 = (bf16[256,1024]{1,0:T(8,128)(2,1)S(1)}, bf16[256,1024]{1,0:T(8,128)(2,1)}, u32[]{:S(2)}, u32[]{:S(2)}) collective-permute-start(bf16[256,1024]{1,0:T(8,128)(2,1)S(1)} %bitcast.135), channel_id=1, source_target_pairs={{0,252},{2,254},{4,0},{6,2},{8,4},{10,6},{12,8},{14,10},{16,12},{1... | collective-permute-start | bytes 1572872 | tf_op jit(solution)/shard_map/ppermute | solution.py:13
  177.3 11.7 %copy-start.4 = (bf16[1024,512]{1,0:T(8,128)(2,1)S(1)}, bf16[1024,512]{1,0:T(8,128)(2,1)}, u32[]{:S(2)}) copy-start(bf16[1024,512]{1,0:T(8,128)(2,1)} %param.10) | copy-start | bytes 3145732
  177.3 42.1 %reduce-scatter.5.cloned.1.call-start = ((), (), s32[]{:S(2)}) async-start(), calls=%async_computation.3 | async-start | bytes 786432 | tf_op jit(solution)/shard_map/reduce_scatter | solution.py:202
  189.1 7.4 %copy-start.5 = (bf16[1024,512]{1,0:T(8,128)(2,1)S(1)}, bf16[1024,512]{1,0:T(8,128)(2,1)}, u32[]{:S(2)}) copy-start(bf16[1024,512]{1,0:T(8,128)(2,1)} %param.11) | copy-start | bytes 3145732
  189.6 7.3 %copy-start.7 = (bf16[1024,512]{1,0:T(8,128)(2,1)S(1)}, bf16[1024,512]{1,0:T(8,128)(2,1)}, u32[]{:S(2)}) copy-start(bf16[1024,512]{1,0:T(8,128)(2,1)} %param.12) | copy-start | bytes 3145732
  (4 other events, 11.8 us)
Sparse Core Ops, SparseCore 0:
  177.5 18.0 reduce-scatter.2
  198.7 20.6 reduce-scatter.4
where the time goes:
time: 231 us; the launch traced here: 226 us
  matrix products  92.3 us (40%)
  local copies, waits for them, and re-layouts  42.9 us (19%)
  waiting for transfers between devices  29.7 us (13%)
  blocking collectives  19.8 us (9%)
  starting transfers between devices  19.3 us (8%)
  between operations  14.7 us (6%)
  other arithmetic  7.75 us (3%)
    dot_general x2, matrix products, key_terms(): jnp.einsum('hqk,qhd->khd', score_grads, spread(block_rows), preferred_ele...  36.8 us
    dot_general x2, matrix products, backward_block(): jnp.einsum('hqk,khd->qhd', score_grads, spread(block_keys), preferred_ele...  23 us
    reduce_scatter x1, waiting for transfers between devices, body(): lax.psum_scatter(partial_in.astype(jnp.bfloat16), 'tp', scatter_dimension...  21.2 us
    ppermute x8, starting transfers between devices, from_behind(): return lax.ppermute(value, axis, pairs)  19.3 us
    concatenate x8, local copies, waits for them, and re-layouts, body(): jnp.concatenate(key_parts + value_parts, axis=2)  15.4 us
    dot_general x1, matrix products, body(): jnp.einsum('bjw,bjtc->wtc', placing, combined, precision=lax.Precision.HI...  10.9 us
    all_gather x1, blocking collectives, body(): grad_whole = lax.all_gather(grad_out, 'tp', axis=1, tiled=True)  10.1 us
    all_gather x1, blocking collectives, body(): whole = lax.all_gather(tokens, 'tp', axis=1, tiled=True)  9.67 us
  transfers between devices with their start and end apart: 10, of which 2 were waited for; matrix products, arithmetic and copies ran while one was open for 20% of the time, Pallas kernels for 0%

commit v1 on v0

v1 whole, which is shorter than its diff:
```python
import functools

import jax
import jax.numpy as jnp
from jax import lax
from jax.experimental import pallas as pl
from jax.experimental.pallas import tpu as pltpu
from jax.sharding import PartitionSpec as P

MESH = pl.DeviceIdType.MESH
BLK = 256
PAIR = 128
NP = 4
HALF = 512
F32 = jnp.float32
BF16 = jnp.bfloat16

SIB, NEAR, FAR, CROSS = 0, 1, 2, 3


def dot(a, b):
    return jnp.dot(a, b, preferred_element_type=F32)


def dot_nt(a, b):
    return lax.dot_general(a, b, (((1,), (1,)), ((), ())), preferred_element_type=F32)


def dot_tn(a, b):
    return lax.dot_general(a, b, (((0,), (0,)), ((), ())), preferred_element_type=F32)


def pick(cond, a, b):
    return lax.select_n(cond, b, a)


def kernel(
    n,
    tok_hbm, wq_hbm, wk_hbm, wv_hbm, wo_hbm, go_hbm, sky_ref, nb_ref, vc_ref,
    out_ref, ig_ref,
    tok, tokp, go, gop, wq, wk, wv, wo, acc,
    kv_own, win, q2, g2, bias, kc, vc, s_ref, d_ref, p_ref, ds_ref,
    att, dq, own_g, near_g, gsib, gfar, gnear, rsib, rnear, rfar, dk, dv,
    osend, orecv, isend, irecv,
    lsem, tp_ssem, tp_rsem, kv_ssem, kv_rsem, g_ssem, g_rsem,
):
    s = lax.axis_index("seq")
    t = lax.axis_index("tp")
    sgn = 1 - 2 * (s % 2)

    def dev(offset):
        return ((s + sgn * offset + n) % n, t)

    sib, near, far, peer = dev(1), dev(2), dev(-2), (s, 1 - t)

    def remote(src, dst, ssem, rsem, to):
        return pltpu.make_async_remote_copy(
            src_ref=src, dst_ref=dst, send_sem=ssem, recv_sem=rsem, device_id=to, device_id_type=MESH
        )

    def local(i, src, dst):
        return pltpu.make_async_copy(src, dst, lsem.at[i])

    loads = [
        local(0, tok_hbm, tok),
        local(1, wk_hbm, wk),
        local(2, wv_hbm, wv),
        local(3, wq_hbm, wq),
        local(4, go_hbm, go),
        local(5, wo_hbm, wo),
    ]
    for copy in loads:
        copy.start()

    barrier = pltpu.get_barrier_semaphore()
    for to in (peer, sib, near, far):
        pl.semaphore_signal(barrier, inc=1, device_id=to, device_id_type=MESH)
    pl.semaphore_wait(barrier, 4)

    def tp_copy(i, src, dst):
        return remote(src, dst, tp_ssem.at[i], tp_rsem.at[i], peer)

    tok_copy = tp_copy(0, tok_hbm, tokp)
    go_copy = tp_copy(1, go_hbm, gop)
    out_copy = tp_copy(2, osend, orecv)
    in_copy = tp_copy(3, isend, irecv)
    tok_copy.start()
    go_copy.start()

    def kv_copy(o, p):
        src = win.at[NEAR, p] if o == CROSS else kv_own.at[p]
        to = {SIB: sib, NEAR: far, FAR: near, CROSS: sib}[o]
        return remote(src, win.at[o, p], kv_ssem.at[o, p], kv_rsem.at[o, p], to)

    def sib_copy(p):
        return remote(gsib.at[p], rsib.at[p], g_ssem.at[0, p], g_rsem.at[0, p], sib)

    def far_copy(p):
        return remote(gfar.at[p], rnear.at[p], g_ssem.at[1, p], g_rsem.at[1, p], far)

    def near_copy(p):
        return remote(gnear.at[p], rfar.at[p], g_ssem.at[2, p], g_rsem.at[2, p], near)

    own_sky = sky_ref[s]
    near_sky = [nb_ref[own_sky, j] for j in range(3)]

    def around(offset):
        sky = sky_ref[(s + sgn * offset + n) % n]
        here = (sky == near_sky[0]) | (sky == near_sky[1]) | (sky == near_sky[2])
        return here, vc_ref[sky]

    own_count = vc_ref[own_sky]
    has_far, far_count = around(-2)
    has_cross, cross_count = around(-1)
    _, sib_count = around(1)
    has_near, near_count = around(2)
    c0 = has_far
    c1 = has_far & has_cross
    c2 = jnp.logical_not(has_near)
    counts = (
        own_count,
        jnp.where(c0, far_count, cross_count),
        jnp.where(c1, cross_count, sib_count),
        jnp.where(c2, sib_count, near_count),
    )
    rows = lax.broadcasted_iota(jnp.int32, (BLK, PAIR), 0)
    for j in range(4):
        bias[j * BLK : (j + 1) * BLK, :] = jnp.where(rows < counts[j], 0.0, -jnp.inf).astype(F32)

    own_rows = pl.ds(pl.multiple_of(t * HALF, HALF), HALF)
    peer_rows = pl.ds(pl.multiple_of((1 - t) * HALF, HALF), HALF)

    loads[0].wait()
    loads[1].wait()
    acc[0] = dot(tok[...], wk[own_rows, :])
    loads[2].wait()
    acc[1] = dot(tok[...], wv[own_rows, :])
    loads[3].wait()
    acc[2] = dot(tok[...], wq[own_rows, :])
    tok_copy.wait_recv()
    for half in range(2):
        cols = slice(half * 256, half * 256 + 256)
        for j, w in ((0, wk), (1, wv)):
            value = (acc[j, :, cols] + dot(tokp[...], w[peer_rows, cols])).astype(BF16)
            kv_own[2 * half, j] = value[:, :PAIR]
            kv_own[2 * half + 1, j] = value[:, PAIR:]
        for p in (2 * half, 2 * half + 1):
            for o in (NEAR, FAR, SIB):
                kv_copy(o, p).start()

    first = lax.broadcasted_iota(jnp.int32, (BLK, PAIR), 1) < 64

    def split(ref, value):
        for p in range(NP):
            part = value[:, p * PAIR : (p + 1) * PAIR]
            ref[p, :BLK, :] = jnp.where(first, part, 0.0).astype(BF16)
            ref[p, BLK:, :] = jnp.where(first, 0.0, part).astype(BF16)

    split(q2, (acc[2] + dot(tokp[...], wq[peer_rows, :])) * 0.125)
    loads[4].wait()
    loads[5].wait()
    acc[0] = dot_nt(go[...], wo[:, own_rows])
    go_copy.wait_recv()
    split(g2, acc[0] + dot_nt(gop[...], wo[:, peer_rows]))

    def forward_near(p):
        kv_copy(NEAR, p).wait_recv()
        kv_copy(CROSS, p).start()

    def combine_near(p):
        sib_copy(p).wait_recv()
        for j in range(2):
            gnear[p, j] = (near_g[p, j] + rsib[p, 1, j].astype(F32)).astype(BF16)
        near_copy(p).start()

    def pair_step(p):
        kv_copy(SIB, p).wait_recv()
        kv_copy(FAR, p).wait_recv()
        kv_copy(CROSS, p).wait_recv()
        for j, ref in ((0, kc), (1, vc)):
            ref[0:256, :] = kv_own[p, j]
            ref[256:512, :] = pick(c0, win[FAR, p, j], win[CROSS, p, j])
            ref[512:768, :] = pick(c1, win[CROSS, p, j], win[SIB, p, j])
            ref[768:1024, :] = pick(c2, win[SIB, p, j], win[NEAR, p, j])
        q = q2[p]
        g = g2[p]
        for k in range(4):
            ks = slice(k * BLK, (k + 1) * BLK)
            b = bias[ks, :]
            s_ref[ks, :] = dot_nt(kc[ks, :], q) + jnp.concatenate([b, b, b, b], axis=1)
            d_ref[ks, :] = dot_nt(vc[ks, :], g)
        for c in range(4):
            cols = slice(c * 128, (c + 1) * 128)
            top = jnp.max(s_ref[:, cols], axis=0, keepdims=True)
            total = jnp.zeros((8, 128), F32)
            mixed = jnp.zeros((8, 128), F32)
            for k in range(8):
                ks = slice(k * 128, (k + 1) * 128)
                e = jnp.exp(s_ref[ks, cols] - top)
                s_ref[ks, cols] = e
                total = total + jnp.sum(e.reshape(16, 8, 128), axis=0)
                mixed = mixed + jnp.sum((e * d_ref[ks, cols]).reshape(16, 8, 128), axis=0)
            inverse = 1.0 / jnp.sum(total, axis=0, keepdims=True)
            delta = jnp.sum(mixed, axis=0, keepdims=True) * inverse
            for k in range(8):
                ks = slice(k * 128, (k + 1) * 128)
                prob = s_ref[ks, cols] * inverse
                p_ref[ks, cols] = prob.astype(BF16)
                ds_ref[ks, cols] = (prob * (d_ref[ks, cols] - delta)).astype(BF16)

        def parts(j, left, right):
            def block(b):
                return dot(left[b * BLK : (b + 1) * BLK, :], right)

            own_g[p, j] = block(0)
            a, b, c = block(1), block(2), block(3)
            zero = jnp.zeros_like(a)
            gfar[p, j] = pick(c0, a, zero).astype(BF16)
            gsib[p, 1, j] = pick(c0, pick(c1, b, zero), a).astype(BF16)
            gsib[p, 0, j] = pick(c1, pick(c2, c, zero), b).astype(BF16)
            near_g[p, j] = pick(c2, zero, c)

        parts(0, ds_ref, q)
        parts(1, p_ref, g)
        sib_copy(p).start()
        far_copy(p).start()
        lanes = pl.ds(pl.multiple_of(p * PAIR, PAIR), PAIR)
        for source, left, ref, scale in ((p_ref, vc, att, 1.0), (ds_ref, kc, dq, 0.125)):
            both = dot_tn(left[...], source[...])
            joined = jnp.concatenate([both[:64, :BLK], both[64:, BLK:]], axis=0) * scale
            ref[:, lanes] = joined.T.astype(BF16)

    forward_near(0)

    @pl.loop(0, NP)
    def _(p):
        @pl.when(p + 1 < NP)
        def _():
            forward_near(p + 1)

        pair_step(p)
        combine_near(p)

    osend[...] = dot(att[...], wo[:, peer_rows]).astype(BF16)
    out_copy.start()
    acc[0] = dot(att[...], wo[:, own_rows])
    acc[1] = dot_nt(dq[...], wq[peer_rows, :])
    acc[2] = dot_nt(dq[...], wq[own_rows, :])

    for p in range(NP):
        far_copy(p).wait_recv()
        near_copy(p).wait_recv()
        lanes = slice(p * PAIR, (p + 1) * PAIR)
        for j, ref in ((0, dk), (1, dv)):
            summed = own_g[p, j] + rsib[p, 0, j].astype(F32)
            summed = summed + rnear[p, j].astype(F32) + rfar[p, j].astype(F32)
            ref[:, lanes] = summed.astype(BF16)
    isend[...] = (
        acc[1] + dot_nt(dk[...], wk[peer_rows, :]) + dot_nt(dv[...], wv[peer_rows, :])
    ).astype(BF16)
    in_copy.start()
    out_copy.wait_recv()
    out_ref[...] = (acc[0] + orecv[...].astype(F32)).astype(BF16)
    acc[1] = acc[2] + dot_nt(dk[...], wk[own_rows, :]) + dot_nt(dv[...], wv[own_rows, :])
    in_copy.wait_recv()
    ig_ref[...] = (acc[1] + irecv[...].astype(F32)).astype(BF16)

    for copy in (tok_copy, go_copy, out_copy, in_copy):
        copy.wait_send()
    for p in range(NP):
        for o in range(4):
            kv_copy(o, p).wait_send()
        for copy in (sib_copy(p), far_copy(p), near_copy(p)):
            copy.wait_send()


def body(n, *args):
    wide = (BLK, HALF)
    half = pltpu.VMEM(wide, BF16)
    weight = pltpu.VMEM((2 * HALF, HALF), BF16)
    pair_kv = pltpu.VMEM((NP, 2, BLK, PAIR), BF16)
    pair_f32 = pltpu.VMEM((NP, 2, BLK, PAIR), F32)
    sib_kv = pltpu.VMEM((NP, 2, 2, BLK, PAIR), BF16)
    scratch = [
        half, half, half, half, weight, weight, weight, pltpu.VMEM((HALF, 2 * HALF), BF16),
        pltpu.VMEM((3,) + wide, F32),
        pair_kv, pltpu.VMEM((4, NP, 2, BLK, PAIR), BF16),
        pltpu.VMEM((NP, 2 * BLK, PAIR), BF16), pltpu.VMEM((NP, 2 * BLK, PAIR), BF16),
        pltpu.VMEM((4 * BLK, PAIR), F32),
        pltpu.VMEM((4 * BLK, PAIR), BF16), pltpu.VMEM((4 * BLK, PAIR), BF16),
        pltpu.VMEM((4 * BLK, 2 * BLK), F32), pltpu.VMEM((4 * BLK, 2 * BLK), F32),
        pltpu.VMEM((4 * BLK, 2 * BLK), BF16), pltpu.VMEM((4 * BLK, 2 * BLK), BF16),
        half, half, pair_f32, pair_f32, sib_kv, pair_kv, pair_kv, sib_kv, pair_kv, pair_kv, half, half,
        half, half, half, half,
        pltpu.SemaphoreType.DMA((6,)),
        pltpu.SemaphoreType.DMA((4,)), pltpu.SemaphoreType.DMA((4,)),
        pltpu.SemaphoreType.DMA((4, NP)), pltpu.SemaphoreType.DMA((4, NP)),
        pltpu.SemaphoreType.DMA((3, NP)), pltpu.SemaphoreType.DMA((3, NP)),
    ]
    shape = jax.ShapeDtypeStruct(wide, BF16)
    return pl.pallas_call(
        functools.partial(kernel, n),
        name="sky_attention",
        out_shape=(shape, shape),
        in_specs=[pl.BlockSpec(memory_space=pl.ANY)] * 6 + [pl.BlockSpec(memory_space=pltpu.SMEM)] * 3,
        out_specs=[pl.BlockSpec(memory_space=pltpu.VMEM)] * 2,
        scratch_shapes=scratch,
        compiler_params=pltpu.CompilerParams(
            collective_id=0, has_side_effects=True, vmem_limit_bytes=48 << 20
        ),
    )(*args)


def solution(mesh):
    placed = (
        P("seq", "tp"),
        P(None, "tp"),
        P(None, "tp"),
        P(None, "tp"),
        P("tp", None),
        P("seq", "tp"),
        P(),
        P(),
        P(),
    )
    return jax.shard_map(
        functools.partial(body, mesh.shape["seq"]),
        mesh=mesh,
        in_specs=placed,
        out_specs=(P("seq", "tp"), P("seq", "tp")),
        check_vma=False,
    )
```

time: 231 us -> 77.8 us (0.34)
  the two profiles are of different devices: /device:TPU:1 before, /device:TPU:229 now
where the time goes in v1:
time: 77.8 us; the launch traced here: 77.4 us
  Pallas kernels  67.8 us (87%)
  local copies, waits for them, and re-layouts  9.01 us (12%)
    pallas_call x1, Pallas kernels, body(): pl.pallas_call(functools.partial(kernel, n), name='sky_attention', out_sh...  67.8 us
    unnamed x19, local copies, waits for them, and re-layouts  9.01 us

profile of v1, /device:TPU:229, one launch (start us, length us, event | category | flops | bytes accessed | tf_op | source)
XLA Modules:
  0.0 77.4 jit_solution(11912937112759767955)
XLA Ops:
  0.6 0.0 copy-start.7
  0.6 0.0 copy-start.6
  0.7 0.8 %copy.11.nb_ref = s32[128,3]{1,0:T(8,128)S(1)} copy(s32[128,3]{0,1:T(4,128)} %param.16) | data formatting | bytes 3072 | tf_op args[7]
  1.4 0.0 copy-done.7
  1.5 0.0 copy-done.6
  1.5 0.0 copy-start
  1.5 1.2 %copy-done = bf16[1024,512]{1,0:T(8,128)(2,1)S(1)} copy-done((bf16[1024,512]{1,0:T(8,128)(2,1)S(1)}, bf16[1024,512]{1,0:T(8,128)(2,1)}, u32[]{:S(2)}) %copy-start) | copy-done | bytes 1048600
  2.7 0.0 copy-start.1
  2.7 1.2 %copy-done.1 = bf16[1024,512]{1,0:T(8,128)(2,1)S(1)} copy-done((bf16[1024,512]{1,0:T(8,128)(2,1)S(1)}, bf16[1024,512]{1,0:T(8,128)(2,1)}, u32[]{:S(2)}) %copy-start.1) | copy-done | bytes 1048600
  3.9 0.0 copy-start.2
  3.9 1.2 %copy-done.2 = bf16[1024,512]{1,0:T(8,128)(2,1)S(1)} copy-done((bf16[1024,512]{1,0:T(8,128)(2,1)S(1)}, bf16[1024,512]{1,0:T(8,128)(2,1)}, u32[]{:S(2)}) %copy-start.2) | copy-done | bytes 1048600
  5.1 0.0 copy-start.3
  5.1 1.2 %copy-done.3 = bf16[512,1024]{1,0:T(8,128)(2,1)S(1)} copy-done((bf16[512,1024]{1,0:T(8,128)(2,1)S(1)}, bf16[512,1024]{1,0:T(8,128)(2,1)}, u32[]{:S(2)}) %copy-start.3) | copy-done | bytes 1048600
  6.4 0.0 copy-start.4
  6.4 0.9 %copy-done.4 = bf16[256,512]{1,0:T(8,128)(2,1)S(1)} copy-done((bf16[256,512]{1,0:T(8,128)(2,1)S(1)}, bf16[256,512]{1,0:T(8,128)(2,1)}, u32[]{:S(2)}) %copy-start.4) | copy-done | bytes 262168
  7.3 0.0 copy-start.5
  7.3 0.9 %copy-done.5 = bf16[256,512]{1,0:T(8,128)(2,1)S(1)} copy-done((bf16[256,512]{1,0:T(8,128)(2,1)S(1)}, bf16[256,512]{1,0:T(8,128)(2,1)}, u32[]{:S(2)}) %copy-start.5) | copy-done | bytes 262168
  8.3 67.8 %sky_attention.1 = (bf16[256,512]{1,0:T(8,128)(2,1)S(1)}, bf16[256,512]{1,0:T(8,128)(2,1)S(1)}) custom-call(bf16[256,512]{1,0:T(8,128)(2,1)S(1)} %copy-done.4, bf16[1024,512]{1,0:T(8,128)(2,1)S(1)} %copy-done, bf16[1024,512]{1,0:T(8,128)(2,1)S(1)} %copy-done.1, bf16[1024,512]{1,0:T(8,128)(2,1)S(1)} %copy-done.2, bf16[512,1024]{1,0:T(8,128)(2,1)S(1)} %copy-done.3, ...), custom_call_target="tpu_custom_call" | custom-call | tf_op jit(solution)/shard_map/sky_attention/pallas_call | solution.py:301
  76.0 0.7 copy.14
  76.7 0.7 copy.15
Async XLA Ops:
  0.6 0.8 %copy-start.7 = (s32[128]{0:T(128)S(1)}, s32[128]{0:T(128)}, u32[]{:S(2)}) copy-start(s32[128]{0:T(128)} %vc_ref.1) | copy-start | bytes 1540
  0.6 0.8 %copy-start.6 = (s32[128]{0:T(128)S(1)}, s32[128]{0:T(128)}, u32[]{:S(2)}) copy-start(s32[128]{0:T(128)} %sky_ref.1) | copy-start | bytes 1540
  1.5 1.2 %copy-start = (bf16[1024,512]{1,0:T(8,128)(2,1)S(1)}, bf16[1024,512]{1,0:T(8,128)(2,1)}, u32[]{:S(2)}) copy-start(bf16[1024,512]{1,0:T(8,128)(2,1)} %wq_hbm.1) | copy-start | bytes 3145732
  2.7 1.2 %copy-start.1 = (bf16[1024,512]{1,0:T(8,128)(2,1)S(1)}, bf16[1024,512]{1,0:T(8,128)(2,1)}, u32[]{:S(2)}) copy-start(bf16[1024,512]{1,0:T(8,128)(2,1)} %wk_hbm.1) | copy-start | bytes 3145732
  3.9 1.2 %copy-start.2 = (bf16[1024,512]{1,0:T(8,128)(2,1)S(1)}, bf16[1024,512]{1,0:T(8,128)(2,1)}, u32[]{:S(2)}) copy-start(bf16[1024,512]{1,0:T(8,128)(2,1)} %wv_hbm.1) | copy-start | bytes 3145732
  5.1 1.2 %copy-start.3 = (bf16[512,1024]{1,0:T(8,128)(2,1)S(1)}, bf16[512,1024]{1,0:T(8,128)(2,1)}, u32[]{:S(2)}) copy-start(bf16[512,1024]{1,0:T(8,128)(2,1)} %wo_hbm.1) | copy-start | bytes 3145732
  6.4 0.9 %copy-start.4 = (bf16[256,512]{1,0:T(8,128)(2,1)S(1)}, bf16[256,512]{1,0:T(8,128)(2,1)}, u32[]{:S(2)}) copy-start(bf16[256,512]{1,0:T(8,128)(2,1)} %tok_hbm.1) | copy-start | bytes 786436
  7.3 0.9 %copy-start.5 = (bf16[256,512]{1,0:T(8,128)(2,1)S(1)}, bf16[256,512]{1,0:T(8,128)(2,1)}, u32[]{:S(2)}) copy-start(bf16[256,512]{1,0:T(8,128)(2,1)} %go_hbm.1) | copy-start | bytes 786436

commit v2 on v1

--- a/solution.py
+++ b/solution.py
@@ -16,6 +16,8 @@
 BF16 = jnp.bfloat16
 
 SIB, NEAR, FAR, CROSS = 0, 1, 2, 3
+KV_RELAYED = (1, 3)
+G_RELAYED = (0, 2)
 
 
 def dot(a, b):
@@ -41,8 +43,8 @@
     tok, tokp, go, gop, wq, wk, wv, wo, acc,
     kv_own, win, q2, g2, bias, kc, vc, s_ref, d_ref, p_ref, ds_ref,
     att, dq, own_g, near_g, gsib, gfar, gnear, rsib, rnear, rfar, dk, dv,
-    osend, orecv, isend, irecv,
-    lsem, tp_ssem, tp_rsem, kv_ssem, kv_rsem, g_ssem, g_rsem,
+    osend, orecv, isend, irecv, kv_relay, g_relay,
+    relay_ssem, relay_rsem, lsem, tp_ssem, tp_rsem, kv_ssem, kv_rsem, g_ssem, g_rsem,
 ):
     s = lax.axis_index("seq")
     t = lax.axis_index("tp")
@@ -52,6 +54,17 @@
         return ((s + sgn * offset + n) % n, t)
 
     sib, near, far, peer = dev(1), dev(2), dev(-2), (s, 1 - t)
+
+    half_n = n // 2
+    right_end = s % half_n >= half_n - 2
+    left_end = s % half_n < 2
+    even = s % 2 == 0
+    near_crosses = (even & right_end) | (jnp.logical_not(even) & left_end)
+    far_crosses = (even & left_end) | (jnp.logical_not(even) & right_end)
+    at_end = right_end | left_end
+    step = jnp.where(right_end, 2, -2)
+    partner = ((s + half_n) % n, t)
+    partners_end = ((s + half_n + step + n) % n, t)
 
     def remote(src, dst, ssem, rsem, to):
         return pltpu.make_async_remote_copy(
@@ -75,7 +88,17 @@
     barrier = pltpu.get_barrier_semaphore()
     for to in (peer, sib, near, far):
         pl.semaphore_signal(barrier, inc=1, device_id=to, device_id_type=MESH)
-    pl.semaphore_wait(barrier, 4)
+
+    @pl.when(at_end)
+    def _():
+        for to in (partner, partners_end):
+            pl.semaphore_signal(barrier, inc=1, device_id=to, device_id_type=MESH)
+        pl.semaphore_wait(barrier, 6)
+
+    @pl.when(jnp.logical_not(at_end))
+    def _():
+        pl.semaphore_wait(barrier, 4)
+
 
     def tp_copy(i, src, dst):
         return remote(src, dst, tp_ssem.at[i], tp_rsem.at[i], peer)
@@ -101,8 +124,57 @@
     def near_copy(p):
         return remote(gnear.at[p], rfar.at[p], g_ssem.at[2, p], g_rsem.at[2, p], near)
 
+    class Crossing:
+        def __init__(self, crosses, direct, first, second):
+            self.crosses, self.direct, self.first, self.second = crosses, direct, first, second
+
+        def start(self):
+            pl.when(self.crosses)(lambda: self.first().start())
+            pl.when(jnp.logical_not(self.crosses))(lambda: self.direct().start())
+
+        def pass_on(self):
+            @pl.when(self.crosses)
+            def _():
+                self.first().wait_recv()
+                self.second().start()
+
+        def wait_send(self):
+            @pl.when(self.crosses)
+            def _():
+                self.first().wait_send()
+                self.second().wait_send()
+
+            pl.when(jnp.logical_not(self.crosses))(lambda: self.direct().wait_send())
+
+    def crossing(crosses, i, direct, src, buffer, dst, sem):
+        return Crossing(
+            crosses,
+            direct,
+            lambda: remote(src, buffer, relay_ssem.at[i], relay_rsem.at[i], partner),
+            lambda: remote(buffer, dst, relay_ssem.at[i + 4], sem, partners_end),
+        )
+
+    def kv_crossing(o, i):
+        p = KV_RELAYED[i]
+        return crossing(
+            near_crosses if o == FAR else far_crosses, i, lambda: kv_copy(o, p),
+            kv_own.at[p], kv_relay.at[i], win.at[o, p], kv_rsem.at[o, p],
+        )
+
+    def g_crossing(is_near, i):
+        p = G_RELAYED[i]
+        if is_near:
+            return crossing(
+                near_crosses, i + 2, lambda: near_copy(p),
+                gnear.at[p], g_relay.at[i], rfar.at[p], g_rsem.at[2, p],
+            )
+        return crossing(
+            far_crosses, i + 2, lambda: far_copy(p),
+            gfar.at[p], g_relay.at[i], rnear.at[p], g_rsem.at[1, p],
+        )
+
     own_sky = sky_ref[s]
-    near_sky = [nb_ref[own_sky, j] for j in range(3)]
+    near_sky = [nb_ref[j, own_sky] for j in range(3)]
 
     def around(offset):
         sky = sky_ref[(s + sgn * offset + n) % n]
@@ -145,8 +217,12 @@
             kv_own[2 * half, j] = value[:, :PAIR]
             kv_own[2 * half + 1, j] = value[:, PAIR:]
         for p in (2 * half, 2 * half + 1):
-            for o in (NEAR, FAR, SIB):
-                kv_copy(o, p).start()
+            for o in (NEAR, FAR):
+                if p in KV_RELAYED:
+                    kv_crossing(o, KV_RELAYED.index(p)).start()
+                else:
+                    kv_copy(o, p).start()
+            kv_copy(SIB, p).start()
 
     first = lax.broadcasted_iota(jnp.int32, (BLK, PAIR), 1) < 64
 
@@ -157,6 +233,8 @@
             ref[p, BLK:, :] = jnp.where(first, 0.0, part).astype(BF16)
 
     split(q2, (acc[2] + dot(tokp[...], wq[peer_rows, :])) * 0.125)
+    for o in (NEAR, FAR):
+        kv_crossing(o, 0).pass_on()
     loads[4].wait()
     loads[5].wait()
     acc[0] = dot_nt(go[...], wo[:, own_rows])
@@ -171,7 +249,16 @@
         sib_copy(p).wait_recv()
         for j in range(2):
             gnear[p, j] = (near_g[p, j] + rsib[p, 1, j].astype(F32)).astype(BF16)
-        near_copy(p).start()
+
+    def send_on(p, is_near):
+        relayed = False
+        for i, r in enumerate(G_RELAYED):
+            pl.when(p == r)(lambda i=i: g_crossing(is_near, i).start())
+            relayed = relayed | (p == r)
+
+        @pl.when(jnp.logical_not(relayed))
+        def _():
+            (near_copy(p) if is_near else far_copy(p)).start()
 
     def pair_step(p):
         kv_copy(SIB, p).wait_recv()
@@ -223,7 +310,7 @@
         parts(0, ds_ref, q)
         parts(1, p_ref, g)
         sib_copy(p).start()
-        far_copy(p).start()
+        send_on(p, False)
         lanes = pl.ds(pl.multiple_of(p * PAIR, PAIR), PAIR)
         for source, left, ref, scale in ((p_ref, vc, att, 1.0), (ds_ref, kc, dq, 0.125)):
             both = dot_tn(left[...], source[...])
@@ -238,8 +325,20 @@
         def _():
             forward_near(p + 1)
 
+        @pl.when(p == 0)
+        def _():
+            for o in (NEAR, FAR):
+                kv_crossing(o, 1).pass_on()
+
         pair_step(p)
         combine_near(p)
+        send_on(p, True)
+        for i in range(2):
+
+            @pl.when(p == G_RELAYED[i] + 1)
+            def _():
+                for is_near in (True, False):
+                    g_crossing(is_near, i).pass_on()
 
     osend[...] = dot(att[...], wo[:, peer_rows]).astype(BF16)
     out_copy.start()
@@ -269,12 +368,20 @@
         copy.wait_send()
     for p in range(NP):
         for o in range(4):
-            kv_copy(o, p).wait_send()
-        for copy in (sib_copy(p), far_copy(p), near_copy(p)):
-            copy.wait_send()
+            if p in KV_RELAYED and o in (NEAR, FAR):
+                kv_crossing(o, KV_RELAYED.index(p)).wait_send()
+            else:
+                kv_copy(o, p).wait_send()
+        sib_copy(p).wait_send()
+        for is_near in (True, False):
+            if p in G_RELAYED:
+                g_crossing(is_near, G_RELAYED.index(p)).wait_send()
+            else:
+                (near_copy(p) if is_near else far_copy(p)).wait_send()
 
 
 def body(n, *args):
+    args = args[:7] + (args[7].T,) + args[8:]
     wide = (BLK, HALF)
     half = pltpu.VMEM(wide, BF16)
     weight = pltpu.VMEM((2 * HALF, HALF), BF16)
@@ -292,6 +399,8 @@
         pltpu.VMEM((4 * BLK, 2 * BLK), BF16), pltpu.VMEM((4 * BLK, 2 * BLK), BF16),
         half, half, pair_f32, pair_f32, sib_kv, pair_kv, pair_kv, sib_kv, pair_kv, pair_kv, half, half,
         half, half, half, half,
+        pltpu.VMEM((2, 2, BLK, PAIR), BF16), pltpu.VMEM((2, 2, BLK, PAIR), BF16),
+        pltpu.SemaphoreType.DMA((8,)), pltpu.SemaphoreType.DMA((4,)),
         pltpu.SemaphoreType.DMA((6,)),
         pltpu.SemaphoreType.DMA((4,)), pltpu.SemaphoreType.DMA((4,)),
         pltpu.SemaphoreType.DMA((4, NP)), pltpu.SemaphoreType.DMA((4, NP)),
@@ -302,11 +411,11 @@
         functools.partial(kernel, n),
         name="sky_attention",
         out_shape=(shape, shape),
-        in_specs=[pl.BlockSpec(memory_space=pl.ANY)] * 6 + [pl.BlockSpec(memory_space=pltpu.SMEM)] * 3,
+        in_specs=[pl.BlockSpec(memory_space=pltpu.HBM)] * 6 + [pl.BlockSpec(memory_space=pltpu.SMEM)] * 3,
         out_specs=[pl.BlockSpec(memory_space=pltpu.VMEM)] * 2,
         scratch_shapes=scratch,
         compiler_params=pltpu.CompilerParams(
-            collective_id=0, has_side_effects=True, vmem_limit_bytes=48 << 20
+            collective_id=0, has_side_effects=True, vmem_limit_bytes=60 << 20
         ),
     )(*args)
 

time: 77.8 us -> 69.9 us (0.90)
  the two profiles are of different devices: /device:TPU:229 before, /device:TPU:1 now
where the time goes in v2:
time: 69.9 us; the launch traced here: 68.7 us
  Pallas kernels  65.6 us (94%)
  local copies, waits for them, and re-layouts  2.42 us (3%)
    pallas_call x1, Pallas kernels, body(): pl.pallas_call(functools.partial(kernel, n), name='sky_attention', out_sh...  65.6 us
    unnamed x4, local copies, waits for them, and re-layouts  2.42 us

profile of v2, /device:TPU:1, one launch (start us, length us, event | category | flops | bytes accessed | tf_op | source)
XLA Modules:
  0.0 68.7 jit_solution(11123093925285953555)
XLA Ops:
  0.6 65.6 %sky_attention.1 = (bf16[256,512]{1,0:T(8,128)(2,1)}, bf16[256,512]{1,0:T(8,128)(2,1)}) custom-call(bf16[256,512]{1,0:T(8,128)(2,1)} %tok_hbm.1, bf16[1024,512]{1,0:T(8,128)(2,1)} %wq_hbm.1, bf16[1024,512]{1,0:T(8,128)(2,1)} %wk_hbm.1, bf16[1024,512]{1,0:T(8,128)(2,1)} %wv_hbm.1, bf16[512,1024]{1,0:T(8,128)(2,1)} %wo_hbm.1, bf16[256,512]{1,0:T(8,128)(2,1)} %go_hbm.1, ...), custom_call_target="tpu_custom_call" | custom-call | tf_op jit(solution)/shard_map/sky_attention/pallas_call | solution.py:410
  66.2 0.0 copy-start
  66.2 1.7 %copy.13 = bf16[256,512]{1,0:T(8,128)(2,1)} copy(bf16[256,512]{1,0:T(8,128)(2,1)} %get-tuple-element.4) | data formatting | bytes 524288
  68.0 0.0 copy-done
  68.0 0.7 %copy.14 = bf16[256,512]{1,0:T(8,128)(2,1)} copy(bf16[256,512]{1,0:T(8,128)(2,1)S(1)} %copy-done) | data formatting | bytes 524288
Async XLA Ops:
  66.2 1.7 %copy-start = (bf16[256,512]{1,0:T(8,128)(2,1)S(1)}, bf16[256,512]{1,0:T(8,128)(2,1)}, u32[]{:S(2)}) copy-start(bf16[256,512]{1,0:T(8,128)(2,1)} %get-tuple-element.5) | copy-start | bytes 786436

commit v3 on v1

--- a/solution.py
+++ b/solution.py
@@ -53,6 +53,13 @@
 
     sib, near, far, peer = dev(1), dev(2), dev(-2), (s, 1 - t)
 
+    half_n = n // 2
+    right_end = s % half_n >= half_n - 2
+    left_end = s % half_n < 2
+    even = s % 2 == 0
+    near_crosses = (even & right_end) | (jnp.logical_not(even) & left_end)
+    far_crosses = (even & left_end) | (jnp.logical_not(even) & right_end)
+
     def remote(src, dst, ssem, rsem, to):
         return pltpu.make_async_remote_copy(
             src_ref=src, dst_ref=dst, send_sem=ssem, recv_sem=rsem, device_id=to, device_id_type=MESH
@@ -102,7 +109,7 @@
         return remote(gnear.at[p], rfar.at[p], g_ssem.at[2, p], g_rsem.at[2, p], near)
 
     own_sky = sky_ref[s]
-    near_sky = [nb_ref[own_sky, j] for j in range(3)]
+    near_sky = [nb_ref[j, own_sky] for j in range(3)]
 
     def around(offset):
         sky = sky_ref[(s + sgn * offset + n) % n]
@@ -145,8 +152,9 @@
             kv_own[2 * half, j] = value[:, :PAIR]
             kv_own[2 * half + 1, j] = value[:, PAIR:]
         for p in (2 * half, 2 * half + 1):
-            for o in (NEAR, FAR, SIB):
-                kv_copy(o, p).start()
+            for o, crosses in ((NEAR, far_crosses), (FAR, near_crosses)):
+                pl.when(jnp.logical_not(crosses))(lambda o=o, p=p: kv_copy(o, p).start())
+            kv_copy(SIB, p).start()
 
     first = lax.broadcasted_iota(jnp.int32, (BLK, PAIR), 1) < 64
 
@@ -161,6 +169,14 @@
     loads[5].wait()
     acc[0] = dot_nt(go[...], wo[:, own_rows])
     go_copy.wait_recv()
+
+    for o, crosses in ((NEAR, far_crosses), (FAR, near_crosses)):
+
+        @pl.when(crosses)
+        def _():
+            for p in range(NP):
+                kv_copy(o, p).start()
+
     split(g2, acc[0] + dot_nt(gop[...], wo[:, peer_rows]))
 
     def forward_near(p):
@@ -171,7 +187,6 @@
         sib_copy(p).wait_recv()
         for j in range(2):
             gnear[p, j] = (near_g[p, j] + rsib[p, 1, j].astype(F32)).astype(BF16)
-        near_copy(p).start()
 
     def pair_step(p):
         kv_copy(SIB, p).wait_recv()
@@ -220,6 +235,7 @@
             gsib[p, 0, j] = pick(c1, pick(c2, c, zero), b).astype(BF16)
             near_g[p, j] = pick(c2, zero, c)
 
+        between(p)
         parts(0, ds_ref, q)
         parts(1, p_ref, g)
         sib_copy(p).start()
@@ -232,14 +248,24 @@
 
     forward_near(0)
 
-    @pl.loop(0, NP)
-    def _(p):
+    def finish(p):
+        combine_near(p)
+        near_copy(p).start()
+
+    def between(p):
         @pl.when(p + 1 < NP)
         def _():
             forward_near(p + 1)
 
+        @pl.when(p > 0)
+        def _():
+            finish(p - 1)
+
+    @pl.loop(0, NP)
+    def _(p):
         pair_step(p)
-        combine_near(p)
+
+    finish(NP - 1)
 
     osend[...] = dot(att[...], wo[:, peer_rows]).astype(BF16)
     out_copy.start()
@@ -275,6 +301,7 @@
 
 
 def body(n, *args):
+    args = args[:7] + (args[7].T,) + args[8:]
     wide = (BLK, HALF)
     half = pltpu.VMEM(wide, BF16)
     weight = pltpu.VMEM((2 * HALF, HALF), BF16)
@@ -302,11 +329,11 @@
         functools.partial(kernel, n),
         name="sky_attention",
         out_shape=(shape, shape),
-        in_specs=[pl.BlockSpec(memory_space=pl.ANY)] * 6 + [pl.BlockSpec(memory_space=pltpu.SMEM)] * 3,
+        in_specs=[pl.BlockSpec(memory_space=pltpu.HBM)] * 6 + [pl.BlockSpec(memory_space=pltpu.SMEM)] * 3,
         out_specs=[pl.BlockSpec(memory_space=pltpu.VMEM)] * 2,
         scratch_shapes=scratch,
         compiler_params=pltpu.CompilerParams(
-            collective_id=0, has_side_effects=True, vmem_limit_bytes=48 << 20
+            collective_id=0, has_side_effects=True, vmem_limit_bytes=60 << 20
         ),
     )(*args)
 

time: 77.8 us -> 63.5 us (0.82)
  the two profiles are of different devices: /device:TPU:229 before, /device:TPU:1 now
where the time goes in v3:
time: 63.5 us; the launch traced here: 62.8 us
  Pallas kernels  59.7 us (94%)
  local copies, waits for them, and re-layouts  2.42 us (4%)
  between operations  0.65 us (1%)
    pallas_call x1, Pallas kernels, body(): pl.pallas_call(functools.partial(kernel, n), name='sky_attention', out_sh...  59.7 us
    unnamed x4, local copies, waits for them, and re-layouts  2.42 us

profile of v3, /device:TPU:1, one launch (start us, length us, event | category | flops | bytes accessed | tf_op | source)
XLA Modules:
  0.0 62.8 jit_solution(5886941586882100444)
XLA Ops:
  0.6 59.7 %sky_attention.1 = (bf16[256,512]{1,0:T(8,128)(2,1)}, bf16[256,512]{1,0:T(8,128)(2,1)}) custom-call(bf16[256,512]{1,0:T(8,128)(2,1)} %tok_hbm.1, bf16[1024,512]{1,0:T(8,128)(2,1)} %wq_hbm.1, bf16[1024,512]{1,0:T(8,128)(2,1)} %wk_hbm.1, bf16[1024,512]{1,0:T(8,128)(2,1)} %wv_hbm.1, bf16[512,1024]{1,0:T(8,128)(2,1)} %wo_hbm.1, bf16[256,512]{1,0:T(8,128)(2,1)} %go_hbm.1, ...), custom_call_target="tpu_custom_call" | custom-call | tf_op jit(solution)/shard_map/sky_attention/pallas_call | solution.py:328
  60.4 0.0 copy-start
  60.4 1.7 %copy.13 = bf16[256,512]{1,0:T(8,128)(2,1)} copy(bf16[256,512]{1,0:T(8,128)(2,1)} %get-tuple-element.4) | data formatting | bytes 524288
  62.1 0.0 copy-done
  62.1 0.7 %copy.14 = bf16[256,512]{1,0:T(8,128)(2,1)} copy(bf16[256,512]{1,0:T(8,128)(2,1)S(1)} %copy-done) | data formatting | bytes 524288
Async XLA Ops:
  60.4 1.7 %copy-start = (bf16[256,512]{1,0:T(8,128)(2,1)S(1)}, bf16[256,512]{1,0:T(8,128)(2,1)}, u32[]{:S(2)}) copy-start(bf16[256,512]{1,0:T(8,128)(2,1)} %get-tuple-element.5) | copy-start | bytes 786436

commit v4 on v3

--- a/solution.py
+++ b/solution.py
@@ -333,7 +333,7 @@
         out_specs=[pl.BlockSpec(memory_space=pltpu.VMEM)] * 2,
         scratch_shapes=scratch,
         compiler_params=pltpu.CompilerParams(
-            collective_id=0, has_side_effects=True, vmem_limit_bytes=60 << 20
+            collective_id=0, has_side_effects=True, vmem_limit_bytes=213 << 18
         ),
     )(*args)
 

time: 63.5 us -> 62.7 us (0.987)
  Pallas kernels: 59.7 us -> 58.7 us
    pallas_call x1, Pallas kernels: 59.7 us -> 58.7 us  [body(): pl.pallas_call(functools.partial(kernel, n), name='sky_attention', out_sh...]
    unnamed x4 -> x8, local copies, waits for them, and re-layouts: 2.42 us -> 2.74 us
where the time goes in v4:
time: 62.7 us; the launch traced here: 62.1 us
  Pallas kernels  58.7 us (94%)
  local copies, waits for them, and re-layouts  2.74 us (4%)
  between operations  0.66 us (1%)
    pallas_call x1, Pallas kernels, body(): pl.pallas_call(functools.partial(kernel, n), name='sky_attention', out_sh...  58.7 us
    unnamed x8, local copies, waits for them, and re-layouts  2.74 us

profile of v4, /device:TPU:1, one launch (start us, length us, event | category | flops | bytes accessed | tf_op | source)
XLA Modules:
  0.0 62.1 jit_solution(18047366916283172314)
XLA Ops:
  0.6 0.0 copy-start.2
  0.6 0.0 copy-start.1
  0.7 0.6 %copy-done.2 = s32[128]{0:T(128)S(1)} copy-done((s32[128]{0:T(128)S(1)}, s32[128]{0:T(128)}, u32[]{:S(2)}) %copy-start.2) | copy-done | bytes 536
  1.3 0.0 copy-done.1
  1.3 0.0 copy-start
  1.3 0.7 %copy-done = s32[128,3]{0,1:T(4,128)S(1)} copy-done((s32[128,3]{0,1:T(4,128)S(1)}, s32[128,3]{0,1:T(4,128)}, u32[]{:S(2)}) %copy-start) | copy-done | bytes 1560
  2.0 58.7 %sky_attention.1 = (bf16[256,512]{1,0:T(8,128)(2,1)S(1)}, bf16[256,512]{1,0:T(8,128)(2,1)S(1)}) custom-call(bf16[256,512]{1,0:T(8,128)(2,1)} %tok_hbm.1, bf16[1024,512]{1,0:T(8,128)(2,1)} %wq_hbm.1, bf16[1024,512]{1,0:T(8,128)(2,1)} %wk_hbm.1, bf16[1024,512]{1,0:T(8,128)(2,1)} %wv_hbm.1, bf16[512,1024]{1,0:T(8,128)(2,1)} %wo_hbm.1, bf16[256,512]{1,0:T(8,128)(2,1)} %go_hbm.1, ...), custom_call_target="tpu_custom_call" | custom-call | tf_op jit(solution)/shard_map/sky_attention/pallas_call | solution.py:328
  60.7 0.7 %copy.13 = bf16[256,512]{1,0:T(8,128)(2,1)} copy(bf16[256,512]{1,0:T(8,128)(2,1)S(1)} %get-tuple-element.4) | data formatting | bytes 524288
  61.4 0.7 %copy.14 = bf16[256,512]{1,0:T(8,128)(2,1)} copy(bf16[256,512]{1,0:T(8,128)(2,1)S(1)} %get-tuple-element.5) | data formatting | bytes 524288
Async XLA Ops:
  0.6 0.7 %copy-start.2 = (s32[128]{0:T(128)S(1)}, s32[128]{0:T(128)}, u32[]{:S(2)}) copy-start(s32[128]{0:T(128)} %vc_ref.1) | copy-start | bytes 1540
  0.6 0.7 %copy-start.1 = (s32[128]{0:T(128)S(1)}, s32[128]{0:T(128)}, u32[]{:S(2)}) copy-start(s32[128]{0:T(128)} %sky_ref.1) | copy-start | bytes 1540
  1.3 0.7 %copy-start = (s32[128,3]{0,1:T(4,128)S(1)}, s32[128,3]{0,1:T(4,128)}, u32[]{:S(2)}) copy-start(s32[128,3]{0,1:T(4,128)} %param.16) | copy-start | bytes 4612

commit v5 on v4

--- a/solution.py
+++ b/solution.py
@@ -302,6 +302,7 @@
 
 def body(n, *args):
     args = args[:7] + (args[7].T,) + args[8:]
+    args = args[:6] + tuple(pltpu.with_memory_space_constraint(x, pltpu.HBM) for x in args[6:])
     wide = (BLK, HALF)
     half = pltpu.VMEM(wide, BF16)
     weight = pltpu.VMEM((2 * HALF, HALF), BF16)

time: 62.7 us -> 61.6 us (0.982)
  local copies, waits for them, and re-layouts: 2.74 us -> 1.41 us
    unnamed x8 -> x2, local copies, waits for them, and re-layouts: 2.74 us -> 1.41 us
where the time goes in v5:
time: 61.6 us; the launch traced here: 61 us
  Pallas kernels  58.9 us (96%)
  local copies, waits for them, and re-layouts  1.41 us (2%)
  between operations  0.64 us (1%)
    pallas_call x1, Pallas kernels, body(): pl.pallas_call(functools.partial(kernel, n), name='sky_attention', out_sh...  58.9 us
    unnamed x2, local copies, waits for them, and re-layouts  1.41 us

profile of v5, /device:TPU:1, one launch (start us, length us, event | category | flops | bytes accessed | tf_op | source)
XLA Modules:
  0.0 61.0 jit_solution(13948761749218116101)
XLA Ops:
  0.6 58.9 %sky_attention.1 = (bf16[256,512]{1,0:T(8,128)(2,1)S(1)}, bf16[256,512]{1,0:T(8,128)(2,1)S(1)}) custom-call(bf16[256,512]{1,0:T(8,128)(2,1)} %tok_hbm.1, bf16[1024,512]{1,0:T(8,128)(2,1)} %wq_hbm.1, bf16[1024,512]{1,0:T(8,128)(2,1)} %wk_hbm.1, bf16[1024,512]{1,0:T(8,128)(2,1)} %wv_hbm.1, bf16[512,1024]{1,0:T(8,128)(2,1)} %wo_hbm.1, bf16[256,512]{1,0:T(8,128)(2,1)} %go_hbm.1, ...), custom_call_target="tpu_custom_call" | custom-call | tf_op jit(solution)/shard_map/sky_attention/pallas_call | solution.py:329
  59.6 0.7 %copy.13 = bf16[256,512]{1,0:T(8,128)(2,1)} copy(bf16[256,512]{1,0:T(8,128)(2,1)S(1)} %get-tuple-element.4) | data formatting | bytes 524288
  60.3 0.7 %copy.14 = bf16[256,512]{1,0:T(8,128)(2,1)} copy(bf16[256,512]{1,0:T(8,128)(2,1)S(1)} %get-tuple-element.5) | data formatting | bytes 524288

commit v6 on v5

--- a/solution.py
+++ b/solution.py
@@ -90,7 +90,8 @@
     tok_copy = tp_copy(0, tok_hbm, tokp)
     go_copy = tp_copy(1, go_hbm, gop)
     out_copy = tp_copy(2, osend, orecv)
-    in_copy = tp_copy(3, isend, irecv)
+    parts_of = [slice(0, BLK // 2), slice(BLK // 2, BLK)]
+    in_copies = [tp_copy(3 + i, isend.at[part], irecv.at[part]) for i, part in enumerate(parts_of)]
     tok_copy.start()
     go_copy.start()
 
@@ -281,17 +282,19 @@
             summed = own_g[p, j] + rsib[p, 0, j].astype(F32)
             summed = summed + rnear[p, j].astype(F32) + rfar[p, j].astype(F32)
             ref[:, lanes] = summed.astype(BF16)
-    isend[...] = (
-        acc[1] + dot_nt(dk[...], wk[peer_rows, :]) + dot_nt(dv[...], wv[peer_rows, :])
-    ).astype(BF16)
-    in_copy.start()
+    for part, copy in zip(parts_of, in_copies):
+        isend[part, :] = (
+            acc[1, part, :] + dot_nt(dk[part, :], wk[peer_rows, :]) + dot_nt(dv[part, :], wv[peer_rows, :])
+        ).astype(BF16)
+        copy.start()
     out_copy.wait_recv()
     out_ref[...] = (acc[0] + orecv[...].astype(F32)).astype(BF16)
     acc[1] = acc[2] + dot_nt(dk[...], wk[own_rows, :]) + dot_nt(dv[...], wv[own_rows, :])
-    in_copy.wait_recv()
-    ig_ref[...] = (acc[1] + irecv[...].astype(F32)).astype(BF16)
-
-    for copy in (tok_copy, go_copy, out_copy, in_copy):
+    for part, copy in zip(parts_of, in_copies):
+        copy.wait_recv()
+        ig_ref[part, :] = (acc[1, part, :] + irecv[part, :].astype(F32)).astype(BF16)
+
+    for copy in (tok_copy, go_copy, out_copy, *in_copies):
         copy.wait_send()
     for p in range(NP):
         for o in range(4):
@@ -321,7 +324,7 @@
         half, half, pair_f32, pair_f32, sib_kv, pair_kv, pair_kv, sib_kv, pair_kv, pair_kv, half, half,
         half, half, half, half,
         pltpu.SemaphoreType.DMA((6,)),
-        pltpu.SemaphoreType.DMA((4,)), pltpu.SemaphoreType.DMA((4,)),
+        pltpu.SemaphoreType.DMA((5,)), pltpu.SemaphoreType.DMA((5,)),
         pltpu.SemaphoreType.DMA((4, NP)), pltpu.SemaphoreType.DMA((4, NP)),
         pltpu.SemaphoreType.DMA((3, NP)), pltpu.SemaphoreType.DMA((3, NP)),
     ]

time: 61.6 us -> 61.7 us (level)
  no operation moved by 1% of the time
where the time goes in v6:
time: 61.7 us; the launch traced here: 61 us
  Pallas kernels  59 us (96%)
  local copies, waits for them, and re-layouts  1.41 us (2%)
  between operations  0.64 us (1%)
    pallas_call x1, Pallas kernels, body(): pl.pallas_call(functools.partial(kernel, n), name='sky_attention', out_sh...  59 us
    unnamed x2, local copies, waits for them, and re-layouts  1.41 us

profile of v6, /device:TPU:1, one launch (start us, length us, event | category | flops | bytes accessed | tf_op | source)
XLA Modules:
  0.0 61.0 jit_solution(6952151116417220180)
XLA Ops:
  0.6 59.0 %sky_attention.1 = (bf16[256,512]{1,0:T(8,128)(2,1)S(1)}, bf16[256,512]{1,0:T(8,128)(2,1)S(1)}) custom-call(bf16[256,512]{1,0:T(8,128)(2,1)} %tok_hbm.1, bf16[1024,512]{1,0:T(8,128)(2,1)} %wq_hbm.1, bf16[1024,512]{1,0:T(8,128)(2,1)} %wk_hbm.1, bf16[1024,512]{1,0:T(8,128)(2,1)} %wv_hbm.1, bf16[512,1024]{1,0:T(8,128)(2,1)} %wo_hbm.1, bf16[256,512]{1,0:T(8,128)(2,1)} %go_hbm.1, ...), custom_call_target="tpu_custom_call" | custom-call | tf_op jit(solution)/shard_map/sky_attention/pallas_call | solution.py:332
  59.6 0.7 %copy.13 = bf16[256,512]{1,0:T(8,128)(2,1)} copy(bf16[256,512]{1,0:T(8,128)(2,1)S(1)} %get-tuple-element.4) | data formatting | bytes 524288
  60.3 0.7 %copy.14 = bf16[256,512]{1,0:T(8,128)(2,1)} copy(bf16[256,512]{1,0:T(8,128)(2,1)S(1)} %get-tuple-element.5) | data formatting | bytes 524288
